TPU v7x, 32 devices: a whole 2x2x4 slice. The times are simulated.
32 devices in a mesh: group: 2 (over y), ctx: 4 (over z), smp: 2 (over x), head: 2 (over core).
Axes of the slice: x: 2, y: 2, z: 4, core: 2. Of those that a mesh axis runs over, the one named last changes fastest.
Arguments:
- queries: bfloat16 [512, 2, 4096], P(('group', 'smp'), 'head'), parts along dimension 0, may hold values from -8 to 8
- prefix_cache: bfloat16 [2, 8192, 2, 512], P(None, ('group', 'ctx'), 'head'), parts along dimension 1, may hold values from -8 to 8
- suffix_cache: bfloat16 [2, 512, 128, 2, 512], P(None, ('group', 'ctx', 'smp'), None, 'head'), parts along dimension 1, may hold values from -8 to 8
- suffix_length: int32 [512], P(('group', 'smp')), parts along dimension 0, may hold values from 1 to 128, as said below
- cache_sample: int32 [512], P('group'), parts along dimension 0, may hold values from 0 to 255, as said below
- residual: bfloat16 [512, 8192], P(('group', 'ctx', 'head'), 'smp'), parts along dimension 0, may hold values from -6 to 6
- w_out: bfloat16 [2, 4096, 8192], P('head', 'ctx', 'smp'), may hold values from -0.75 to 0.75
- norm_gain: float32 [8192], P('smp'), may hold values from 0.1 to 1.9
- gate_matrix: bfloat16 [8192, 16384], P('smp', ('ctx', 'head')), may hold values from -0.0625 to 0.0625
- w_up: bfloat16 [8192, 16384], P('smp', ('ctx', 'head')), may hold values from -0.0625 to 0.0625
- w_down: bfloat16 [16384, 8192], P(('ctx', 'head'), 'smp'), may hold values from -0.046875 to 0.046875
Outputs:
- mixed: bfloat16 [512, 8192], P(('group', 'ctx', 'head'), 'smp'), parts along dimension 0
There are 2 independent parts, one for each index of `group`. A program takes and returns all parts, laid end to end along the dimension named above; an argument that names none is the same for every part. Nothing has to cross between parts.
Inputs may be any that keep to these rules, and one draw needn't show every extreme that they name: `suffix_length`: the longest is exactly 128 in every draw. A permutation; cache row r and sample cache_sample[r] lie in the same group, the group of row r being (r // 32) % (2) and that of sample i being i // 128.
All inputs are finite; a program needn't handle non-finite values.
Results may differ from a plain program's by a relative error of at most 0.012.
Values may be sent and summed in bfloat16 or wider, within the bound.
A program may use at most 192 MiB of HBM per device.

v0:
```python
import jax
import jax.numpy as jnp
from jax import lax
from jax.sharding import PartitionSpec as P

D = 8192
QUERY_HEADS = 64
KEY_VALUE_HEADS = 8
HD = 128
EPSILON = 1e-05


def suffix_piece(row_queries, suffix_cache, row_lengths, key_value_heads_here, score_scale):
    rows_here = suffix_cache.shape[1]
    suffix_keys = suffix_cache[0].reshape(rows_here, -1, key_value_heads_here, HD)
    suffix_values = suffix_cache[1].reshape(rows_here, -1, key_value_heads_here, HD)
    row_scores = (
        jnp.einsum("rjgd,rtjd->rjgt", row_queries, suffix_keys, preferred_element_type=jnp.float32)
        * score_scale
    )
    positions = lax.broadcasted_iota(jnp.int32, row_scores.shape, 3)
    row_scores = jnp.where(positions < row_lengths[:, None, None, None], row_scores, -jnp.inf)
    row_high = jnp.max(row_scores, axis=3)
    row_weights = jnp.exp(row_scores - row_high[..., None])
    row_totals = jnp.sum(row_weights, axis=3)
    row_summed = jnp.einsum(
        "rjgt,rtjd->rjgd",
        row_weights.astype(jnp.bfloat16),
        suffix_values,
        preferred_element_type=jnp.float32,
    )
    row_output = (row_summed / row_totals[..., None]).astype(jnp.bfloat16)
    return (row_output, row_high + jnp.log(row_totals))


def merge_pieces(pieces):
    piece_values, piece_lse = pieces
    item_count = piece_values.shape[0]
    peak = jnp.max(piece_lse, axis=1, keepdims=True)
    piece_weights = jnp.exp(piece_lse - peak)
    shaped = piece_values.reshape(item_count, piece_values.shape[1], piece_lse.shape[2], HD)
    numer = jnp.sum(piece_weights[..., None] * shaped, axis=1)
    denom = jnp.sum(piece_weights, axis=1)
    return (numer / denom[..., None]).reshape(item_count, -1).astype(jnp.bfloat16)


def activate(gate_sum, up_sum, square_sum):
    factor = lax.rsqrt(square_sum / D + EPSILON)[:, None]
    return (jax.nn.silu(factor * gate_sum) * (factor * up_sum)).astype(jnp.bfloat16)


def on_device(
    queries,
    prefix_cache,
    suffix_cache,
    suffix_length,
    cache_sample,
    residual,
    w_out,
    norm_gain,
    gate_matrix,
    w_up,
    w_down,
):
    group_rows = queries.shape[0]
    key_value_heads_here = prefix_cache.shape[3] // HD
    queries_per_key_value = QUERY_HEADS // KEY_VALUE_HEADS
    heads_local = key_value_heads_here * queries_per_key_value
    score_scale = HD ** (-0.5)
    queries_split = queries.reshape(group_rows, key_value_heads_here, queries_per_key_value, HD)
    prefix_keys = prefix_cache[0].reshape(-1, key_value_heads_here, HD)
    prefix_values = prefix_cache[1].reshape(-1, key_value_heads_here, HD)
    scores = (
        jnp.einsum("sjgd,pjd->jsgp", queries_split, prefix_keys, preferred_element_type=jnp.float32)
        * score_scale
    )
    highest = jnp.max(scores, axis=3)
    weights = jnp.exp(scores - highest[..., None])
    totals = jnp.sum(weights, axis=3)
    summed = jnp.einsum(
        "jsgp,pjd->sjgd",
        weights.astype(jnp.bfloat16),
        prefix_values,
        preferred_element_type=jnp.float32,
    )
    prefix_out = (summed / jnp.transpose(totals, (1, 0, 2))[..., None]).astype(jnp.bfloat16)
    prefix_lse = jnp.transpose(highest + jnp.log(totals), (1, 0, 2))
    rows_here = suffix_cache.shape[1]
    flat_index = lax.axis_index("ctx") * lax.axis_size("smp") + lax.axis_index("smp")
    row_ids = lax.dynamic_slice_in_dim(cache_sample, flat_index * rows_here, rows_here, 0)
    local_ids = row_ids % group_rows
    row_queries = jnp.take(queries_split, local_ids, axis=0)
    row_lengths = jnp.take(suffix_length, local_ids, axis=0)
    suffix_out, suffix_lse = suffix_piece(
        row_queries, suffix_cache, row_lengths, key_value_heads_here, score_scale
    )
    onehot = (local_ids[None, :] == jnp.arange(group_rows, dtype=jnp.int32)[:, None]).astype(
        jnp.float32
    )
    present = jnp.sum(onehot, axis=1)[:, None]
    placed_out = jnp.dot(
        onehot,
        suffix_out.reshape(rows_here, -1).astype(jnp.float32),
        precision=lax.Precision.HIGHEST,
    )
    placed_lse = jnp.dot(
        onehot, suffix_lse.reshape(rows_here, heads_local), precision=lax.Precision.HIGHEST
    )
    own_lse = prefix_lse.reshape(group_rows, heads_local)
    other_lse = jnp.where(present > 0, placed_lse, own_lse)
    top = jnp.maximum(own_lse, other_lse)
    own_weight = jnp.exp(own_lse - top)
    other_weight = present * jnp.exp(other_lse - top)
    both_weight = own_weight + other_weight
    own_values = prefix_out.reshape(group_rows, heads_local, HD).astype(jnp.float32)
    other_values = placed_out.reshape(group_rows, heads_local, HD)
    local_out = (
        own_weight[..., None] * own_values + other_weight[..., None] * other_values
    ) / both_weight[..., None]
    local_lse = top + jnp.log(both_weight)
    attn_slice = merge_pieces(
        (
            lax.all_to_all(
                local_out.reshape(group_rows, 1, -1), "ctx", split_axis=2, concat_axis=1, tiled=True
            ),
            lax.all_to_all(
                local_lse.reshape(group_rows, 1, -1), "ctx", split_axis=2, concat_axis=1, tiled=True
            ),
        )
    )
    proj_weight = w_out[0]
    all_attn = lax.all_gather(attn_slice, "smp", axis=0, tiled=True)
    own_state = (
        residual.astype(jnp.float32)
        + lax.psum_scatter(
            jnp.dot(all_attn, proj_weight, preferred_element_type=jnp.float32),
            ("ctx", "head"),
            scatter_dimension=0,
            tiled=True,
        )
    ).astype(jnp.bfloat16)
    state = lax.all_gather(own_state, ("ctx", "head"), axis=0, tiled=True)
    state_wide = state.astype(jnp.float32)
    square_part = jnp.sum(state_wide * state_wide, axis=1)
    scaled = (state_wide * norm_gain).astype(jnp.bfloat16)
    gate_portion = jnp.dot(scaled, gate_matrix, preferred_element_type=jnp.float32)
    up_part = jnp.dot(scaled, w_up, preferred_element_type=jnp.float32)
    gate_sum, up_sum, square_sum = (
        lax.psum(gate_portion.astype(jnp.bfloat16), "smp").astype(jnp.float32),
        lax.psum(up_part.astype(jnp.bfloat16), "smp").astype(jnp.float32),
        lax.psum(square_part.astype(jnp.bfloat16), "smp").astype(jnp.float32),
    )
    activated = activate(gate_sum, up_sum, square_sum)
    ffn_rows = lax.psum_scatter(
        jnp.dot(activated, w_down, preferred_element_type=jnp.float32).astype(jnp.bfloat16),
        ("ctx", "head"),
        scatter_dimension=0,
        tiled=True,
    ).astype(jnp.float32)
    return (own_state.astype(jnp.float32) + ffn_rows).astype(jnp.bfloat16)


def solution(mesh):
    in_specs = (
        P(("group", "smp"), "head", None),
        P(None, ("group", "ctx"), "head", None),
        P(None, ("group", "ctx", "smp"), None, "head", None),
        P(("group", "smp")),
        P("group"),
        P(("group", "ctx", "head"), "smp"),
        P("head", "ctx", "smp"),
        P("smp"),
        P("smp", ("ctx", "head")),
        P("smp", ("ctx", "head")),
        P(("ctx", "head"), "smp"),
    )
    out_specs = P(("group", "ctx", "head"), "smp")
    return jax.shard_map(
        on_device, mesh=mesh, in_specs=in_specs, out_specs=out_specs, check_vma=False
    )
```

profile of v0, /device:TPU:0, one launch (start us, length us, event | category | flops | bytes accessed | tf_op | source)
XLA Modules:
  0.0 360.2 jit_solution(7161917489603728494)
XLA Ops:
  6.5 1.7 fusion.47
  8.2 0.5 copy.56
  8.8 1.4 copy.60
  10.4 5.9 %fusion.46 = (bf16[1,32,128,1,512]{4,2,3,1,0:T(8,128)(2,1)}, bf16[1,32,128,1,512]{4,2,3,1,0:T(8,128)(2,1)}) fusion(bf16[2,32,128,1,512]{4,2,3,1,0:T(8,128)(2,1)} %param.13), kind=kLoop, calls=%fused_computation.77 | loop fusion | bytes 16777216 | tf_op jit(solution)/shard_map/slice | solution.py:16
  16.4 6.4 %copy.57 = bf16[1,32,128,1,512]{2,4,1,3,0:T(8,128)(2,1)} copy(bf16[1,32,128,1,512]{4,2,3,1,0:T(8,128)(2,1)} %get-tuple-element.18) | data formatting | bytes 8388608
  22.8 8.1 %multiply_reduce_fusion = (f32[4,128,8]{1,2,0:T(8,128)S(1)}, f32[4,128,8,1024]{3,1,2,0:T(8,128)}) fusion(bf16[1024,4,128,1]{0,2,3,1:T(8,128)(2,1)S(1)} %bitcast.92, bf16[128,4,8,128]{3,2,1,0:T(8,128)(2,1)S(1)} %bitcast.89), kind=kOutput, calls=%fused_computation.3 | convolution fusion | flops 1082126336 | bytes 18890752 | tf_op jit(solution)/shard_map/sjgd,pjd->jsgp/dot_general | solution.py:74
  30.9 0.6 gather_fusion.1
  31.5 0.7 gather_fusion
  32.2 3.5 fusion.48
  36.4 7.7 %fusion.1 = f32[4,128,8]{1,2,0:T(8,128)S(1)} fusion(f32[4,128,8,1024]{3,1,2,0:T(8,128)} %get-tuple-element.22, f32[4,128,8]{1,2,0:T(8,128)S(1)} %get-tuple-element.21), kind=kLoop, calls=%fused_computation.5 | loop fusion | flops 12578816 | bytes 16809984 | tf_op jit(solution)/shard_map/reduce_sum | solution.py:79
  44.0 0.8 log_add_fusion
  44.9 6.3 %all-to-all-start = ((f32[128,1,32]{0,1,2:T(1,128)}), f32[128,1,32]{0,1,2:T(1,128)S(1)}, u32[]{:S(2)}, u32[]{:S(2)}) async-start(f32[128,1,32]{0,1,2:T(1,128)} %bitcast.8), calls=%async_computation | async-start | bytes 32768 | tf_op jit(solution)/shard_map/all_to_all | solution.py:126
  51.2 0.5 copy.45
  51.8 6.4 %copy.58 = bf16[1,32,128,1,512]{2,4,1,3,0:T(8,128)(2,1)} copy(bf16[1,32,128,1,512]{4,2,3,1,0:T(8,128)(2,1)} %get-tuple-element.17) | data formatting | bytes 8388608
  58.2 4.5 %fusion.18 = bf16[32,4,8,128]{3,2,1,0:T(8,128)(2,1)S(1)} fusion(bf16[32,128,4,128]{1,3,2,0:T(8,128)(2,1)} %bitcast.91, f32[32,4,8,128]{3,2,1,0:T(8,128)S(1)} %get-tuple-element.24, f32[32,4,8]{2,1,0:T(4,128)S(1)} %fusion.24, f32[32,4,8]{2,1,0:T(4,128)S(1)} %get-tuple-element.23), kind=kOutput, calls=%fused_computation.28 | convolution fusion | flops 34078720 | bytes 4988928 | tf_op jit(solution)/shard_map/rjgt,rtjd->rjgd/dot_general | solution.py:26
  62.7 7.6 %fusion.12 = bf16[128,4,8,128]{0,3,2,1:T(8,128)(2,1)S(1)} fusion(bf16[1024,4,128,1]{0,2,3,1:T(8,128)(2,1)S(1)} %bitcast.96, f32[4,128,8,1024]{3,1,2,0:T(8,128)} %get-tuple-element.22, f32[4,128,8]{1,2,0:T(8,128)S(1)} %get-tuple-element.21, f32[128,4,8]{0,2,1:T(8,128)S(1)} %bitcast.99), kind=kOutput, calls=%fused_computation.22 | convolution fusion | flops 1087373312 | bytes 18907136 | tf_op jit(solution)/shard_map/jsgp,pjd->sjgd/dot_general | solution.py:80
  70.3 2.0 fusion.11
  72.4 5.1 %all-to-all-start.1 = ((f32[128,1,4096]{0,1,2:T(1,128)}), f32[128,1,4096]{0,1,2:T(1,128)S(1)}, u32[]{:S(2)}, u32[]{:S(2)}) async-start(f32[128,1,4096]{0,1,2:T(1,128)} %bitcast.93), calls=%async_computation.1 | async-start | bytes 4194304 | tf_op jit(solution)/shard_map/all_to_all | solution.py:123
  77.5 47.6 %all-to-all-done.1 = f32[128,1,4096]{0,1,2:T(1,128)S(1)} async-done(((f32[128,1,4096]{0,1,2:T(1,128)}), f32[128,1,4096]{0,1,2:T(1,128)S(1)}, u32[]{:S(2)}, u32[]{:S(2)}) %all-to-all-start.1) | async-done | bytes 2097184 | tf_op jit(solution)/shard_map/all_to_all | solution.py:123
  125.4 8.2 %all_gather.6 = bf16[256,1024]{0,1:T(8,128)(2,1)S(1)} all-gather(bf16[128,1024]{0,1:T(8,128)(2,1)S(1)} %bitcast.94), channel_id=1, replica_groups=mesh['group'=2,'ctx'=4,'smp'=2,'head'=2] {'smp'}, dimensions={0}, use_global_device_ids=true | all-gather | bytes 786432 | tf_op jit(solution)/shard_map/all_gather | solution.py:132
  133.6 7.7 %fusion.4 = f32[256,4096]{1,0:T(8,128)} fusion(bf16[256,1024]{0,1:T(8,128)(2,1)S(1)} %all_gather.6, bf16[1,1024,4096]{2,1,0:T(8,128)(2,1)} %param.17), kind=kOutput, calls=%fused_computation.7 | convolution fusion | flops 2147483648 | bytes 13107200 | tf_op jit(solution)/shard_map/dot_general | solution.py:136
  141.4 48.2 %reduce-scatter.3.cloned.1.call-done = f32[32,4096]{1,0:T(8,128)} async-done(((f32[256,4096]{1,0:T(8,128)}), f32[32,4096]{1,0:T(8,128)}) %reduce-scatter.3.cloned.1.call-update) | async-done | bytes 524304 | tf_op jit(solution)/shard_map/reduce_scatter | solution.py:135
  189.6 1.8 add_convert_fusion.1
  191.5 27.7 %all-gather.2.cloned.1.call-done = bf16[256,4096]{1,0:T(8,128)(2,1)} async-done(((bf16[32,4096]{1,0:T(8,128)(2,1)}), bf16[256,4096]{1,0:T(8,128)(2,1)}) %all-gather.2.cloned.1.call-update) | async-done | bytes 2097168 | tf_op jit(solution)/shard_map/all_gather | solution.py:142
  219.2 12.0 %convolution_convert_fusion.1 = bf16[256,2048]{1,0:T(8,128)(2,1)} fusion(bf16[4096,2048]{1,0:T(8,128)(2,1)} %param.20, bf16[256,4096]{1,0:T(8,128)(2,1)} %all-gather.2.cloned.1.call-done, f32[4096]{0:T(1024)S(1)} %copy-done.6), kind=kOutput, calls=%fused_computation.16 | convolution fusion | flops 4298637312 | bytes 19939328 | tf_op jit(solution)/shard_map/dot_general | solution.py:147
  231.2 9.3 %convolution_convert_fusion.2 = bf16[256,2048]{1,0:T(8,128)(2,1)} fusion(bf16[4096,2048]{1,0:T(8,128)(2,1)} %param.19, bf16[256,4096]{1,0:T(8,128)(2,1)S(1)} %copy-done.3, f32[4096]{0:T(1024)S(1)} %copy-done.6), kind=kOutput, calls=%fused_computation.17 | convolution fusion | flops 4298637312 | bytes 19939328 | tf_op jit(solution)/shard_map/dot_general | solution.py:146
  240.6 0.5 fusion.8
  241.1 5.2 %psum.21 = bf16[256]{0:T(256)(128)(2,1)S(1)} all-reduce(bf16[256]{0:T(256)(128)(2,1)S(1)} %fusion.8), channel_id=1, replica_groups=mesh['group'=2,'ctx'=4,'smp'=2,'head'=2] {'smp'}, use_global_device_ids=true, to_apply=%region_10.11 | all-reduce | flops 256 | bytes 1024 | tf_op jit(solution)/shard_map/psum | solution.py:151
  246.2 56.8 %all-reduce.3.cloned.1.call-done = (bf16[256,2048]{1,0:T(8,128)(2,1)}, bf16[256,2048]{1,0:T(8,128)(2,1)}) async-done(((bf16[256,2048]{1,0:T(8,128)(2,1)}, bf16[256,2048]{1,0:T(8,128)(2,1)}), (bf16[256,2048]{1,0:T(8,128)(2,1)}, bf16[256,2048]{1,0:T(8,128)(2,1)})) %all-reduce.3.cloned.1.call-update) | async-done | bytes 2097168 | tf_op jit(solution)/shard_map/psum | solution.py:150
  303.0 12.6 %convolution_convert_fusion = bf16[256,4096]{1,0:T(8,128)(2,1)} fusion(bf16[2048,4096]{1,0:T(8,128)(2,1)} %param.21, bf16[256,2048]{1,0:T(8,128)(2,1)} %get-tuple-element.5, bf16[256,2048]{1,0:T(8,128)(2,1)} %get-tuple-element.6, f32[256]{0:T(256)S(1)} %add_rsqrt_fusion), kind=kOutput, calls=%fused_computation.13 | convolution fusion | flops 4301258752 | bytes 20972544 | tf_op jit(solution)/shard_map/dot_general | solution.py:155
  315.7 36.3 %reduce-scatter.5.cloned.1.call-done = bf16[32,4096]{1,0:T(8,128)(2,1)} async-done(((bf16[256,4096]{1,0:T(8,128)(2,1)}), bf16[32,4096]{1,0:T(8,128)(2,1)}) %reduce-scatter.5.cloned.1.call-update) | async-done | bytes 262160 | tf_op jit(solution)/shard_map/reduce_scatter | solution.py:154
  352.0 1.7 add_convert_fusion
  (36 shorter events, 1.3 us)
Async XLA Ops:
  6.5 25.0 %copy-start = (s32[128]{0:T(128)S(1)}, s32[128]{0:T(128)}, u32[]{:S(2)}) copy-start(s32[128]{0:T(128)} %param.14) | copy-start | bytes 1540
  6.5 3.7 %copy-start.5 = (s32[256]{0:T(256)S(1)}, s32[256]{0:T(256)}, u32[]{:S(2)}) copy-start(s32[256]{0:T(256)} %param.15) | copy-start | bytes 3076
  44.9 27.5 %all-to-all-start = ((f32[128,1,32]{0,1,2:T(1,128)}), f32[128,1,32]{0,1,2:T(1,128)S(1)}, u32[]{:S(2)}, u32[]{:S(2)}) async-start(f32[128,1,32]{0,1,2:T(1,128)} %bitcast.8), calls=%async_computation | async-start | bytes 32768 | tf_op jit(solution)/shard_map/all_to_all | solution.py:126
  72.4 52.7 %all-to-all-start.1 = ((f32[128,1,4096]{0,1,2:T(1,128)}), f32[128,1,4096]{0,1,2:T(1,128)S(1)}, u32[]{:S(2)}, u32[]{:S(2)}) async-start(f32[128,1,4096]{0,1,2:T(1,128)} %bitcast.93), calls=%async_computation.1 | async-start | bytes 4194304 | tf_op jit(solution)/shard_map/all_to_all | solution.py:123
  77.5 112.2 %reduce-scatter.3.cloned.1.call-start = ((), (), s32[]{:S(2)}) async-start(), calls=%async_computation.4 | async-start | bytes 4718592 | tf_op jit(solution)/shard_map/reduce_scatter | solution.py:135
  141.3 48.3 %copy-start.4 = (bf16[32,4096]{1,0:T(8,128)(2,1)S(1)}, bf16[32,4096]{1,0:T(8,128)(2,1)}, u32[]{:S(2)}) copy-start(bf16[32,4096]{1,0:T(8,128)(2,1)} %param.16) | copy-start | bytes 786436
  141.3 77.9 %copy-start.6 = (f32[4096]{0:T(1024)S(1)}, f32[4096]{0:T(1024)}, u32[]{:S(2)}) copy-start(f32[4096]{0:T(1024)} %param.18) | copy-start | bytes 49156
  141.3 77.9 %all-gather.2.cloned.1.call-start = ((), (), s32[]{:S(2)}) async-start(), calls=%async_computation.5 | async-start | bytes 2359296 | tf_op jit(solution)/shard_map/all_gather | solution.py:142
  191.4 111.6 %all-reduce.3.cloned.1.call-start = ((), (), s32[]{:S(2)}) async-start(), calls=%async_computation.7 | async-start | bytes 4194304 | tf_op jit(solution)/shard_map/psum | solution.py:150
  219.2 12.0 %copy-start.3 = (bf16[256,4096]{1,0:T(8,128)(2,1)S(1)}, bf16[256,4096]{1,0:T(8,128)(2,1)}, u32[]{:S(2)}) copy-start(bf16[256,4096]{1,0:T(8,128)(2,1)} %all-gather.2.cloned.1.call-done) | copy-start | bytes 6291460
  240.5 111.4 %reduce-scatter.5.cloned.1.call-start = ((), (), s32[]{:S(2)}) async-start(), calls=%async_computation.6 | async-start | bytes 2359296 | tf_op jit(solution)/shard_map/reduce_scatter | solution.py:154
  303.0 48.9 %copy-start.2 = (bf16[32,4096]{1,0:T(8,128)(2,1)S(1)}, bf16[32,4096]{1,0:T(8,128)(2,1)}, u32[]{:S(2)}) copy-start(bf16[32,4096]{1,0:T(8,128)(2,1)} %add_convert_fusion.1) | copy-start | bytes 786436
  303.0 50.7 %copy-start.1 = (s32[128]{0:T(128)S(1)}, s32[128]{0:T(128)}, u32[]{:S(2)}) copy-start(s32[128]{0:T(128)} %param.14) | copy-start | bytes 1540
Sparse Core Ops, SparseCore 0:
  141.4 48.1 reduce-scatter.2
  191.6 27.6 all-gather.1
  240.6 62.3 all-reduce.2
  315.8 36.1 reduce-scatter.4
where the time goes:
time: 361 us; the launch traced here: 360 us
  waiting for transfers between devices  217 us (60%)
  matrix products  68.3 us (19%)
  local copies, waits for them, and re-layouts  24.4 us (7%)
  blocking collectives  13.4 us (4%)
  between operations  13.2 us (4%)
  other arithmetic  12.6 us (3%)
  starting transfers between devices  11.6 us (3%)
    psum x1, waiting for transfers between devices, on_device(): lax.psum(up_part.astype(jnp.bfloat16), 'smp').astype(jnp.float32)  56.8 us
    reduce_scatter x1, waiting for transfers between devices, on_device(): lax.psum_scatter(jnp.dot(all_attn, proj_weight, preferred_element_type=jn...  48.2 us
    all_to_all x1, waiting for transfers between devices, on_device(): lax.all_to_all(local_out.reshape(group_rows, 1, -1), 'ctx', split_axis=2,...  47.6 us
    reduce_scatter x1, waiting for transfers between devices, on_device(): lax.psum_scatter(jnp.dot(activated, w_down, preferred_element_type=jnp.fl...  36.3 us
    all_gather x1, waiting for transfers between devices, on_device(): state = lax.all_gather(own_state, ('ctx', 'head'), axis=0, tiled=True)  27.7 us
    unnamed x18, local copies, waits for them, and re-layouts  14.8 us
    dot_general x1, matrix products, on_device(): jnp.dot(activated, w_down, preferred_element_type=jnp.float32)  12.6 us
    dot_general x1, matrix products, on_device(): up_part = jnp.dot(scaled, w_up, preferred_element_type=jnp.float32)  12 us
  transfers between devices with their start and end apart: 6, of which 5 were waited for; matrix products, arithmetic and copies ran while one was open for 6% of the time, Pallas kernels for 0%

commit v1 on v0

--- a/solution.py
+++ b/solution.py
@@ -120,8 +120,18 @@
     local_lse = top + jnp.log(both_weight)
     attn_slice = merge_pieces(
         (
-            lax.all_to_all(
-                local_out.reshape(group_rows, 1, -1), "ctx", split_axis=2, concat_axis=1, tiled=True
+            jnp.concatenate(
+                lax.all_to_all(
+                    jnp.stack(
+                        jnp.split(
+                            local_out.reshape(group_rows, 1, -1), lax.axis_size("ctx"), axis=2
+                        )
+                    ),
+                    "ctx",
+                    0,
+                    0,
+                ),
+                axis=1,
             ),
             lax.all_to_all(
                 local_lse.reshape(group_rows, 1, -1), "ctx", split_axis=2, concat_axis=1, tiled=True

time: 361 us -> 362 us (level)
  no operation moved by 1% of the time
where the time goes in v1:
time: 362 us; the launch traced here: 361 us
  waiting for transfers between devices  217 us (60%)
  matrix products  66.9 us (18%)
  local copies, waits for them, and re-layouts  24.7 us (7%)
  other arithmetic  14.2 us (4%)
  blocking collectives  13.4 us (4%)
  between operations  13.3 us (4%)
  starting transfers between devices  11.6 us (3%)
    psum x1, waiting for transfers between devices, on_device(): lax.psum(up_part.astype(jnp.bfloat16), 'smp').astype(jnp.float32)  56.8 us
    reduce_scatter x1, waiting for transfers between devices, on_device(): lax.psum_scatter(jnp.dot(all_attn, proj_weight, preferred_element_type=jn...  48.2 us
    all_to_all x1, waiting for transfers between devices, on_device(): lax.all_to_all(jnp.stack(jnp.split(local_out.reshape(group_rows, 1, -1),...  47.6 us
    reduce_scatter x1, waiting for transfers between devices, on_device(): lax.psum_scatter(jnp.dot(activated, w_down, preferred_element_type=jnp.fl...  36.2 us
    all_gather x1, waiting for transfers between devices, on_device(): state = lax.all_gather(own_state, ('ctx', 'head'), axis=0, tiled=True)  27.7 us
    unnamed x18, local copies, waits for them, and re-layouts  14.8 us
    dot_general x1, matrix products, on_device(): jnp.dot(activated, w_down, preferred_element_type=jnp.float32)  12.6 us
    dot_general x1, matrix products, on_device(): up_part = jnp.dot(scaled, w_up, preferred_element_type=jnp.float32)  12 us
  transfers between devices with their start and end apart: 6, of which 5 were waited for; matrix products, arithmetic and copies ran while one was open for 6% of the time, Pallas kernels for 0%

profile of v1, /device:TPU:0, one launch (start us, length us, event | category | flops | bytes accessed | tf_op | source)
XLA Modules:
  0.0 360.7 jit_solution(5946010752161462324)
XLA Ops:
  6.5 1.7 fusion.49
  8.2 0.5 copy.54
  8.8 1.4 copy.58
  10.4 5.9 %fusion.48 = (bf16[1,32,128,1,512]{4,2,3,1,0:T(8,128)(2,1)}, bf16[1,32,128,1,512]{4,2,3,1,0:T(8,128)(2,1)}) fusion(bf16[2,32,128,1,512]{4,2,3,1,0:T(8,128)(2,1)} %param.13), kind=kLoop, calls=%fused_computation.84 | loop fusion | bytes 16777216 | tf_op jit(solution)/shard_map/slice | solution.py:16
  16.4 6.4 %copy.55 = bf16[1,32,128,1,512]{2,4,1,3,0:T(8,128)(2,1)} copy(bf16[1,32,128,1,512]{4,2,3,1,0:T(8,128)(2,1)} %get-tuple-element.18) | data formatting | bytes 8388608
  22.8 8.1 %multiply_reduce_fusion = (f32[4,128,8]{1,2,0:T(8,128)S(1)}, f32[4,128,8,1024]{3,1,2,0:T(8,128)}) fusion(bf16[1024,4,128,1]{0,2,3,1:T(8,128)(2,1)S(1)} %bitcast.107, bf16[128,4,8,128]{3,2,1,0:T(8,128)(2,1)S(1)} %bitcast.104), kind=kOutput, calls=%fused_computation.3 | convolution fusion | flops 1082126336 | bytes 18890752 | tf_op jit(solution)/shard_map/sjgd,pjd->jsgp/dot_general | solution.py:74
  30.9 0.6 gather_fusion.1
  31.5 0.7 gather_fusion
  32.2 3.5 fusion.50
  36.4 7.7 %fusion.1 = f32[4,128,8]{1,2,0:T(8,128)S(1)} fusion(f32[4,128,8,1024]{3,1,2,0:T(8,128)} %get-tuple-element.26, f32[4,128,8]{1,2,0:T(8,128)S(1)} %get-tuple-element.25), kind=kLoop, calls=%fused_computation.5 | loop fusion | flops 12578816 | bytes 16809984 | tf_op jit(solution)/shard_map/reduce_sum | solution.py:79
  44.0 0.8 log_add_fusion
  44.9 6.3 %all-to-all-start = ((f32[128,1,32]{0,1,2:T(1,128)}), f32[128,1,32]{0,1,2:T(1,128)S(1)}, u32[]{:S(2)}, u32[]{:S(2)}) async-start(f32[128,1,32]{0,1,2:T(1,128)} %bitcast.8), calls=%async_computation | async-start | bytes 32768 | tf_op jit(solution)/shard_map/all_to_all | solution.py:136
  51.2 0.5 copy.44
  51.8 6.4 %copy.56 = bf16[1,32,128,1,512]{2,4,1,3,0:T(8,128)(2,1)} copy(bf16[1,32,128,1,512]{4,2,3,1,0:T(8,128)(2,1)} %get-tuple-element.17) | data formatting | bytes 8388608
  58.2 4.5 %fusion.19 = bf16[32,4,8,128]{3,2,1,0:T(8,128)(2,1)S(1)} fusion(bf16[32,128,4,128]{1,3,2,0:T(8,128)(2,1)} %bitcast.106, f32[32,4,8,128]{3,2,1,0:T(8,128)S(1)} %get-tuple-element.28, f32[32,4,8]{2,1,0:T(4,128)S(1)} %fusion.26, f32[32,4,8]{2,1,0:T(4,128)S(1)} %get-tuple-element.27), kind=kOutput, calls=%fused_computation.30 | convolution fusion | flops 34078720 | bytes 4988928 | tf_op jit(solution)/shard_map/rjgt,rtjd->rjgd/dot_general | solution.py:26
  62.7 7.6 %fusion.13 = bf16[128,4,8,128]{0,3,2,1:T(8,128)(2,1)S(1)} fusion(bf16[1024,4,128,1]{0,2,3,1:T(8,128)(2,1)S(1)} %bitcast.110, f32[4,128,8,1024]{3,1,2,0:T(8,128)} %get-tuple-element.26, f32[4,128,8]{1,2,0:T(8,128)S(1)} %get-tuple-element.25, f32[128,4,8]{0,2,1:T(8,128)S(1)} %bitcast.113), kind=kOutput, calls=%fused_computation.25 | convolution fusion | flops 1087373312 | bytes 18907136 | tf_op jit(solution)/shard_map/jsgp,pjd->sjgd/dot_general | solution.py:80
  70.3 0.7 fusion.11
  71.2 1.5 pad_maximum_fusion
  72.6 5.1 %all-to-all-start.1 = ((f32[4,128,1,1024]{1,3,2,0:T(8,128)}), f32[4,128,1,1024]{1,3,2,0:T(8,128)S(1)}, u32[]{:S(2)}, u32[]{:S(2)}) async-start(f32[4,128,1,1024]{1,3,2,0:T(8,128)} %pad_maximum_fusion), calls=%async_computation.1 | async-start | bytes 4194304 | tf_op jit(solution)/shard_map/all_to_all | solution.py:124
  77.8 47.6 %all-to-all-done.1 = f32[4,128,1,1024]{1,3,2,0:T(8,128)S(1)} async-done(((f32[4,128,1,1024]{1,3,2,0:T(8,128)}), f32[4,128,1,1024]{1,3,2,0:T(8,128)S(1)}, u32[]{:S(2)}, u32[]{:S(2)}) %all-to-all-start.1) | async-done | bytes 2097184 | tf_op jit(solution)/shard_map/all_to_all | solution.py:124
  125.9 8.2 %all_gather.6 = bf16[256,1024]{0,1:T(8,128)(2,1)S(1)} all-gather(bf16[128,1024]{0,1:T(8,128)(2,1)S(1)} %fusion.24), channel_id=1, replica_groups=mesh['group'=2,'ctx'=4,'smp'=2,'head'=2] {'smp'}, dimensions={0}, use_global_device_ids=true | all-gather | bytes 786432 | tf_op jit(solution)/shard_map/all_gather | solution.py:142
  134.1 7.7 %fusion.4 = f32[256,4096]{1,0:T(8,128)} fusion(bf16[256,1024]{0,1:T(8,128)(2,1)S(1)} %all_gather.6, bf16[1,1024,4096]{2,1,0:T(8,128)(2,1)} %param.17), kind=kOutput, calls=%fused_computation.7 | convolution fusion | flops 2147483648 | bytes 13107200 | tf_op jit(solution)/shard_map/dot_general | solution.py:146
  141.9 48.2 %reduce-scatter.3.cloned.1.call-done = f32[32,4096]{1,0:T(8,128)} async-done(((f32[256,4096]{1,0:T(8,128)}), f32[32,4096]{1,0:T(8,128)}) %reduce-scatter.3.cloned.1.call-update) | async-done | bytes 524304 | tf_op jit(solution)/shard_map/reduce_scatter | solution.py:145
  190.1 1.8 add_convert_fusion.1
  192.0 27.7 %all-gather.2.cloned.1.call-done = bf16[256,4096]{1,0:T(8,128)(2,1)} async-done(((bf16[32,4096]{1,0:T(8,128)(2,1)}), bf16[256,4096]{1,0:T(8,128)(2,1)}) %all-gather.2.cloned.1.call-update) | async-done | bytes 2097168 | tf_op jit(solution)/shard_map/all_gather | solution.py:152
  219.7 12.0 %convolution_convert_fusion.1 = bf16[256,2048]{1,0:T(8,128)(2,1)} fusion(bf16[4096,2048]{1,0:T(8,128)(2,1)} %param.20, bf16[256,4096]{1,0:T(8,128)(2,1)} %all-gather.2.cloned.1.call-done, f32[4096]{0:T(1024)S(1)} %copy-done.6), kind=kOutput, calls=%fused_computation.16 | convolution fusion | flops 4298637312 | bytes 19939328 | tf_op jit(solution)/shard_map/dot_general | solution.py:157
  231.7 9.3 %convolution_convert_fusion.2 = bf16[256,2048]{1,0:T(8,128)(2,1)} fusion(bf16[4096,2048]{1,0:T(8,128)(2,1)} %param.19, bf16[256,4096]{1,0:T(8,128)(2,1)S(1)} %copy-done.3, f32[4096]{0:T(1024)S(1)} %copy-done.6), kind=kOutput, calls=%fused_computation.17 | convolution fusion | flops 4298637312 | bytes 19939328 | tf_op jit(solution)/shard_map/dot_general | solution.py:156
  241.6 5.2 %psum.21 = bf16[256]{0:T(256)(128)(2,1)S(1)} all-reduce(bf16[256]{0:T(256)(128)(2,1)S(1)} %fusion.8), channel_id=1, replica_groups=mesh['group'=2,'ctx'=4,'smp'=2,'head'=2] {'smp'}, use_global_device_ids=true, to_apply=%region_10.11 | all-reduce | flops 256 | bytes 1024 | tf_op jit(solution)/shard_map/psum | solution.py:161
  246.7 56.8 %all-reduce.3.cloned.1.call-done = (bf16[256,2048]{1,0:T(8,128)(2,1)}, bf16[256,2048]{1,0:T(8,128)(2,1)}) async-done(((bf16[256,2048]{1,0:T(8,128)(2,1)}, bf16[256,2048]{1,0:T(8,128)(2,1)}), (bf16[256,2048]{1,0:T(8,128)(2,1)}, bf16[256,2048]{1,0:T(8,128)(2,1)})) %all-reduce.3.cloned.1.call-update) | async-done | bytes 2097168 | tf_op jit(solution)/shard_map/psum | solution.py:160
  303.6 12.6 %convolution_convert_fusion = bf16[256,4096]{1,0:T(8,128)(2,1)} fusion(bf16[2048,4096]{1,0:T(8,128)(2,1)} %param.21, bf16[256,2048]{1,0:T(8,128)(2,1)} %get-tuple-element.5, bf16[256,2048]{1,0:T(8,128)(2,1)} %get-tuple-element.6, f32[256]{0:T(256)S(1)} %add_rsqrt_fusion), kind=kOutput, calls=%fused_computation.13 | convolution fusion | flops 4301258752 | bytes 20972544 | tf_op jit(solution)/shard_map/dot_general | solution.py:165
  316.2 36.2 %reduce-scatter.5.cloned.1.call-done = bf16[32,4096]{1,0:T(8,128)(2,1)} async-done(((bf16[256,4096]{1,0:T(8,128)(2,1)}), bf16[32,4096]{1,0:T(8,128)(2,1)}) %reduce-scatter.5.cloned.1.call-update) | async-done | bytes 262160 | tf_op jit(solution)/shard_map/reduce_scatter | solution.py:164
  352.4 1.7 add_convert_fusion
  (39 shorter events, 2.2 us)
Async XLA Ops:
  6.5 25.0 %copy-start = (s32[128]{0:T(128)S(1)}, s32[128]{0:T(128)}, u32[]{:S(2)}) copy-start(s32[128]{0:T(128)} %param.14) | copy-start | bytes 1540
  6.5 3.7 %copy-start.5 = (s32[256]{0:T(256)S(1)}, s32[256]{0:T(256)}, u32[]{:S(2)}) copy-start(s32[256]{0:T(256)} %param.15) | copy-start | bytes 3076
  44.9 27.8 %all-to-all-start = ((f32[128,1,32]{0,1,2:T(1,128)}), f32[128,1,32]{0,1,2:T(1,128)S(1)}, u32[]{:S(2)}, u32[]{:S(2)}) async-start(f32[128,1,32]{0,1,2:T(1,128)} %bitcast.8), calls=%async_computation | async-start | bytes 32768 | tf_op jit(solution)/shard_map/all_to_all | solution.py:136
  72.6 52.7 %all-to-all-start.1 = ((f32[4,128,1,1024]{1,3,2,0:T(8,128)}), f32[4,128,1,1024]{1,3,2,0:T(8,128)S(1)}, u32[]{:S(2)}, u32[]{:S(2)}) async-start(f32[4,128,1,1024]{1,3,2,0:T(8,128)} %pad_maximum_fusion), calls=%async_computation.1 | async-start | bytes 4194304 | tf_op jit(solution)/shard_map/all_to_all | solution.py:124
  77.7 112.4 %reduce-scatter.3.cloned.1.call-start = ((), (), s32[]{:S(2)}) async-start(), calls=%async_computation.4 | async-start | bytes 4718592 | tf_op jit(solution)/shard_map/reduce_scatter | solution.py:145
  141.8 48.3 %copy-start.4 = (bf16[32,4096]{1,0:T(8,128)(2,1)S(1)}, bf16[32,4096]{1,0:T(8,128)(2,1)}, u32[]{:S(2)}) copy-start(bf16[32,4096]{1,0:T(8,128)(2,1)} %param.16) | copy-start | bytes 786436
  141.8 77.9 %copy-start.6 = (f32[4096]{0:T(1024)S(1)}, f32[4096]{0:T(1024)}, u32[]{:S(2)}) copy-start(f32[4096]{0:T(1024)} %param.18) | copy-start | bytes 49156
  141.8 77.9 %all-gather.2.cloned.1.call-start = ((), (), s32[]{:S(2)}) async-start(), calls=%async_computation.5 | async-start | bytes 2359296 | tf_op jit(solution)/shard_map/all_gather | solution.py:152
  191.9 111.6 %all-reduce.3.cloned.1.call-start = ((), (), s32[]{:S(2)}) async-start(), calls=%async_computation.7 | async-start | bytes 4194304 | tf_op jit(solution)/shard_map/psum | solution.py:160
  219.7 12.0 %copy-start.3 = (bf16[256,4096]{1,0:T(8,128)(2,1)S(1)}, bf16[256,4096]{1,0:T(8,128)(2,1)}, u32[]{:S(2)}) copy-start(bf16[256,4096]{1,0:T(8,128)(2,1)} %all-gather.2.cloned.1.call-done) | copy-start | bytes 6291460
  241.0 111.4 %reduce-scatter.5.cloned.1.call-start = ((), (), s32[]{:S(2)}) async-start(), calls=%async_computation.6 | async-start | bytes 2359296 | tf_op jit(solution)/shard_map/reduce_scatter | solution.py:164
  303.5 48.9 %copy-start.2 = (bf16[32,4096]{1,0:T(8,128)(2,1)S(1)}, bf16[32,4096]{1,0:T(8,128)(2,1)}, u32[]{:S(2)}) copy-start(bf16[32,4096]{1,0:T(8,128)(2,1)} %add_convert_fusion.1) | copy-start | bytes 786436
  303.6 50.6 %copy-start.1 = (s32[128]{0:T(128)S(1)}, s32[128]{0:T(128)}, u32[]{:S(2)}) copy-start(s32[128]{0:T(128)} %param.14) | copy-start | bytes 1540
Sparse Core Ops, SparseCore 0:
  141.9 48.1 reduce-scatter.2
  192.1 27.6 all-gather.1
  241.1 62.3 all-reduce.2
  316.3 36.0 reduce-scatter.4
